TPU v7x, 512 devices: a whole 4x8x8 slice. The times are simulated.
512 devices in a mesh: seq: 256 (over z, x, y_hi, core), head: 2 (over y_lo).
Axes of the slice: x: 4, y: 8 (y_hi: 4, y_lo: 2; y = y_hi * 2 + y_lo), z: 8, core: 2. Of those that a mesh axis runs over, the one named last changes fastest.
Arguments:
- queries: bfloat16 [65536, 1792], P('seq', 'head'), may hold values from -120 to 120
- key_rows: bfloat16 [65536, 256], P('seq', 'head'), may hold values from -9 to 9
- value_rows: bfloat16 [65536, 256], P('seq', 'head'), may hold values from -6 to 6
- out_weight: bfloat16 [1792, 3584], P('head', 'seq'), may hold values from -0.125 to 0.125
Outputs:
- projected: bfloat16 [65536, 3584], P('seq', 'head')
All inputs are finite; a program needn't handle non-finite values.
Results may differ from a plain program's by a relative error of at most 0.009.
Values may be sent and summed in bfloat16 or wider, within the bound.
A program may use at most 64 MiB of HBM per device.

v0:
```python
import functools
import math

import jax
import jax.numpy as jnp
from jax import lax
from jax.sharding import PartitionSpec as P

QPK = 7
HD = 128
BLK = 256


masked_score = -1e30


def padded_2(shard, sides, width):
    for axis, dim in sides:
        devices, length = (lax.axis_size(axis), shard.shape[dim])
        up = [(i, (i + 1) % devices) for i in range(devices - 1)]
        down = [(j, i) for i, j in up]
        last = lax.slice_in_dim(shard, length - width, length, axis=dim)
        first = lax.slice_in_dim(shard, 0, width, axis=dim)
        before = lax.ppermute(last, axis, up)
        after = lax.ppermute(first, axis, down)
        shard = jnp.concatenate([before, shard, after], axis=dim)
    return shard


def partner_2(value, axis, apart):
    mask = 2**apart
    pairs = [(source, source ^ mask) for source in range(lax.axis_size(axis))]
    return lax.ppermute(value, axis, pairs)


def head_partial(key_block, value_block, usable, query_head):
    scores = lax.dot_general(
        query_head, key_block, (((1,), (1,)), ((), ())), preferred_element_type=jnp.float32
    )
    scores = scores * (1.0 / math.sqrt(HD))
    scores = jnp.where(usable[None, :], scores, masked_score)
    peak = jnp.max(scores, axis=1)
    weights = jnp.exp(scores - peak[:, None])
    weight_sum = jnp.sum(weights, axis=1)
    numerator = jnp.dot(
        weights.astype(jnp.bfloat16), value_block, preferred_element_type=jnp.float32
    )
    return (peak, weight_sum, numerator)


def attend(query_block, key_value, usable):
    return lax.map(functools.partial(head_partial, key_value[0], key_value[1], usable), query_block)


def finish(partial_value):
    blended = partial_value[2] / partial_value[1][..., None]
    return jnp.transpose(blended, (1, 0, 2)).reshape(blended.shape[1], -1).astype(jnp.bfloat16)


def block_slice(array, block_slot):
    return array[:, block_slot * BLK : (block_slot + 1) * BLK]


def local(queries, key_rows, value_rows, out_weight):
    token_count = key_rows.shape[0]
    per_dev = token_count // BLK
    seq_count = lax.axis_size("seq")
    device_rank = lax.axis_index("seq")
    remote_bits = seq_count.bit_length() - 1
    query_heads = jnp.transpose(queries.reshape(token_count, QPK, HD), (1, 0, 2))
    key_value = jnp.stack([key_rows, value_rows])
    padded = padded_2(key_value, (("seq", 1),), BLK)
    all_true = jnp.ones((BLK,), dtype=bool)
    lower_usable = jnp.broadcast_to(device_rank > 0, (BLK,))
    upper_usable = jnp.broadcast_to(device_rank < seq_count - 1, (BLK,))
    ordering = [bit_number for bit_number in range(remote_bits) if per_dev << bit_number >= 2]
    partners = [partner_2(key_value, "seq", bit_number) for bit_number in ordering]
    pieces = [block_slice(padded, 0), block_slice(padded, 1), block_slice(padded, 2)]
    validity = [lower_usable, all_true, upper_usable]
    pieces, validity = (pieces, validity)
    pieces = pieces + [block_slice(partner, 0) for partner in partners]
    validity = validity + [all_true for partner in partners]
    partial_value = attend(
        block_slice(query_heads, 0), jnp.concatenate(pieces, 1), jnp.concatenate(validity)
    )
    results = finish(partial_value)
    column_terms = jnp.dot(
        results,
        lax.all_gather(out_weight, "seq", axis=1, tiled=True),
        preferred_element_type=jnp.float32,
    )
    return lax.psum_scatter(
        column_terms.astype(jnp.bfloat16), "head", scatter_dimension=1, tiled=True
    )


def solution(mesh):
    in_specs = (P("seq", "head"), P("seq", "head"), P("seq", "head"), P("head", "seq"))
    out_specs = P("seq", "head")
    return jax.shard_map(local, mesh=mesh, in_specs=in_specs, out_specs=out_specs, check_vma=False)
```

profile of v0, /device:TPU:1, one launch (start us, length us, event | category | flops | bytes accessed | tf_op | source)
XLA Modules:
  0.0 203.3 jit_solution(17513403721721763695)
XLA Ops:
  6.5 0.7 all-gather.3.cloned.1.call-update
  7.3 0.9 pad_maximum_fusion
  8.2 5.6 %collective-permute-start = (bf16[2,256,128]{2,1,0:T(8,128)(2,1)S(1)}, bf16[2,256,128]{2,1,0:T(8,128)(2,1)S(1)}, u32[]{:S(2)}, u32[]{:S(2)}) collective-permute-start(bf16[2,256,128]{2,1,0:T(8,128)(2,1)S(1)} %pad_maximum_fusion), channel_id=1, source_target_pairs={{0,2},{2,4},{4,6},{6,8},{8,10},{10,12},{12,14},{14,16},{16,18},{18... | collective-permute-start | bytes 393224 | tf_op jit(solution)/shard_map/ppermute | solution.py:24
  13.8 10.6 %collective-permute-start.8 = (bf16[2,256,128]{2,1,0:T(8,128)(2,1)S(1)}, bf16[2,256,128]{2,1,0:T(8,128)(2,1)S(1)}, u32[]{:S(2)}, u32[]{:S(2)}) collective-permute-start(bf16[2,256,128]{2,1,0:T(8,128)(2,1)S(1)} %pad_maximum_fusion), channel_id=1, source_target_pairs={{0,256},{2,258},{4,260},{6,262},{8,264},{10,266},{12,268},{14,270}... | collective-permute-start | bytes 393224 | tf_op jit(solution)/shard_map/ppermute | solution.py:33
  24.4 4.0 %collective-permute-start.7 = (bf16[2,256,128]{2,1,0:T(8,128)(2,1)S(1)}, bf16[2,256,128]{2,1,0:T(8,128)(2,1)S(1)}, u32[]{:S(2)}, u32[]{:S(2)}) collective-permute-start(bf16[2,256,128]{2,1,0:T(8,128)(2,1)S(1)} %pad_maximum_fusion), channel_id=1, source_target_pairs={{0,128},{2,130},{4,132},{6,134},{8,136},{10,138},{12,140},{14,142}... | collective-permute-start | bytes 393224 | tf_op jit(solution)/shard_map/ppermute | solution.py:33
  28.5 3.1 %collective-permute-start.6 = (bf16[2,256,128]{2,1,0:T(8,128)(2,1)S(1)}, bf16[2,256,128]{2,1,0:T(8,128)(2,1)S(1)}, u32[]{:S(2)}, u32[]{:S(2)}) collective-permute-start(bf16[2,256,128]{2,1,0:T(8,128)(2,1)S(1)} %pad_maximum_fusion), channel_id=1, source_target_pairs={{0,64},{2,66},{4,68},{6,70},{8,72},{10,74},{12,76},{14,78},{16,80}... | collective-permute-start | bytes 393224 | tf_op jit(solution)/shard_map/ppermute | solution.py:33
  31.6 5.4 %collective-permute-start.2 = (bf16[2,256,128]{2,1,0:T(8,128)(2,1)S(1)}, bf16[2,256,128]{2,1,0:T(8,128)(2,1)S(1)}, u32[]{:S(2)}, u32[]{:S(2)}) collective-permute-start(bf16[2,256,128]{2,1,0:T(8,128)(2,1)S(1)} %pad_maximum_fusion), channel_id=1, source_target_pairs={{0,4},{2,6},{4,0},{6,2},{8,12},{10,14},{12,8},{14,10},{16,20},{18,... | collective-permute-start | bytes 393224 | tf_op jit(solution)/shard_map/ppermute | solution.py:33
  37.0 1.2 copy.8
  38.3 1.9 collective-permute-start.1
  40.3 6.6 %collective-permute-done.1 = bf16[2,256,128]{2,1,0:T(8,128)(2,1)S(1)} collective-permute-done((bf16[2,256,128]{2,1,0:T(8,128)(2,1)S(1)}, bf16[2,256,128]{2,1,0:T(8,128)(2,1)S(1)}, u32[]{:S(2)}, u32[]{:S(2)}) %collective-permute-start.1) | collective-permute-done | bytes 131104 | tf_op jit(solution)/shard_map/ppermute | solution.py:25
  47.0 4.4 %collective-permute-start.3 = (bf16[2,256,128]{2,1,0:T(8,128)(2,1)S(1)}, bf16[2,256,128]{2,1,0:T(8,128)(2,1)S(1)}, u32[]{:S(2)}, u32[]{:S(2)}) collective-permute-start(bf16[2,256,128]{2,1,0:T(8,128)(2,1)S(1)} %pad_maximum_fusion), channel_id=1, source_target_pairs={{0,8},{2,10},{4,12},{6,14},{8,0},{10,2},{12,4},{14,6},{16,24},{18,... | collective-permute-start | bytes 393224 | tf_op jit(solution)/shard_map/ppermute | solution.py:33
  51.4 3.0 %collective-permute-start.4 = (bf16[2,256,128]{2,1,0:T(8,128)(2,1)S(1)}, bf16[2,256,128]{2,1,0:T(8,128)(2,1)S(1)}, u32[]{:S(2)}, u32[]{:S(2)}) collective-permute-start(bf16[2,256,128]{2,1,0:T(8,128)(2,1)S(1)} %pad_maximum_fusion), channel_id=1, source_target_pairs={{0,16},{2,18},{4,20},{6,22},{8,24},{10,26},{12,28},{14,30},{16,0},... | collective-permute-start | bytes 393224 | tf_op jit(solution)/shard_map/ppermute | solution.py:33
  54.4 3.2 %collective-permute-done.3 = bf16[2,256,128]{2,1,0:T(8,128)(2,1)S(1)} collective-permute-done((bf16[2,256,128]{2,1,0:T(8,128)(2,1)S(1)}, bf16[2,256,128]{2,1,0:T(8,128)(2,1)S(1)}, u32[]{:S(2)}, u32[]{:S(2)}) %collective-permute-start.3) | collective-permute-done | bytes 131104 | tf_op jit(solution)/shard_map/ppermute | solution.py:33
  57.6 4.7 %collective-permute-start.5 = (bf16[2,256,128]{2,1,0:T(8,128)(2,1)S(1)}, bf16[2,256,128]{2,1,0:T(8,128)(2,1)S(1)}, u32[]{:S(2)}, u32[]{:S(2)}) collective-permute-start(bf16[2,256,128]{2,1,0:T(8,128)(2,1)S(1)} %pad_maximum_fusion), channel_id=1, source_target_pairs={{0,32},{2,34},{4,36},{6,38},{8,40},{10,42},{12,44},{14,46},{16,48}... | collective-permute-start | bytes 393224 | tf_op jit(solution)/shard_map/ppermute | solution.py:33
  62.4 2.5 %collective-permute-done.5 = bf16[2,256,128]{2,1,0:T(8,128)(2,1)S(1)} collective-permute-done((bf16[2,256,128]{2,1,0:T(8,128)(2,1)S(1)}, bf16[2,256,128]{2,1,0:T(8,128)(2,1)S(1)}, u32[]{:S(2)}, u32[]{:S(2)}) %collective-permute-start.5) | collective-permute-done | bytes 131104 | tf_op jit(solution)/shard_map/ppermute | solution.py:33
  65.0 13.3 %while.12 = (s32[]{:T(128)}, f32[7,256]{1,0:T(8,128)S(1)}, f32[7,256,128]{1,2,0:T(8,128)S(1)}, pred[2560]{0:T(1024)(128)(4,1)S(1)}, bf16[7,256,128]{1,2,0:T(8,12...) while((s32[]{:T(128)}, f32[7,256]{1,0:T(8,128)S(1)}, ...), condition=%wide.region_3.4_spmd, body=%wide.region_0.3_spmd.sunk | while | flops 340131328 | bytes 9380977 | solution.py:52
  66.2 0.7 fusion.31
  67.0 0.6 fusion.29
  68.1 0.7 fusion.31
  68.9 0.6 fusion.29
  70.0 0.7 fusion.31
  70.8 0.6 fusion.29
  71.9 0.7 fusion.31
  73.8 0.7 fusion.31
  74.6 0.6 fusion.29
  75.7 0.7 fusion.31
  76.5 0.6 fusion.29
  77.6 0.7 fusion.31
  78.4 68.3 %all-gather.3.cloned.1.call-done = bf16[256,14,896]{2,1,0:T(8,128)(2,1)} async-done(((bf16[1,14,896]{2,1,0:T(8,128)(2,1)}), bf16[256,14,896]{2,1,0:T(8,128)(2,1)}) %all-gather.3.cloned.1.call-update) | async-done | bytes 6422544 | tf_op jit(solution)/shard_map/all_gather | solution.py:89
  146.8 10.7 %reshape.10 = bf16[3584,896]{1,0:T(8,128)(2,1)} reshape(bf16[256,14,896]{2,1,0:T(8,128)(2,1)} %all-gather.3.cloned.1.call-done) | data formatting | bytes 12845056
  157.5 6.2 %convolution_convert_fusion = bf16[256,3584]{1,0:T(8,128)(2,1)} fusion(bf16[256,896]{0,1:T(8,128)(2,1)S(1)} %bitcast.42, bf16[3584,896]{1,0:T(8,128)(2,1)} %reshape.10), kind=kOutput, calls=%fused_computation.12 | convolution fusion | flops 1645084672 | bytes 8716288 | tf_op jit(solution)/shard_map/dot_general | solution.py:87
  163.7 32.7 %reduce-scatter.2.cloned.1.call-done = bf16[256,1792]{1,0:T(8,128)(2,1)} async-done(((bf16[256,3584]{1,0:T(8,128)(2,1)}), bf16[256,1792]{1,0:T(8,128)(2,1)}) %reduce-scatter.2.cloned.1.call-update) | async-done | bytes 917520 | tf_op jit(solution)/shard_map/reduce_scatter | solution.py:92
  (48 shorter events, 5.6 us)
Async XLA Ops:
  6.5 33.8 %copy-start = (bf16[256,128]{1,0:T(8,128)(2,1)S(1)}, bf16[256,128]{1,0:T(8,128)(2,1)}, u32[]{:S(2)}) copy-start(bf16[256,128]{1,0:T(8,128)(2,1)} %param.8) | copy-start | bytes 196612
  6.5 33.8 %copy-start.1 = (bf16[256,128]{1,0:T(8,128)(2,1)S(1)}, bf16[256,128]{1,0:T(8,128)(2,1)}, u32[]{:S(2)}) copy-start(bf16[256,128]{1,0:T(8,128)(2,1)} %param.7) | copy-start | bytes 196612
  6.5 140.2 %all-gather.3.cloned.1.call-start = ((), (), s32[]{:S(2)}) async-start(), calls=%async_computation.2 | async-start | bytes 7368704 | tf_op jit(solution)/shard_map/all_gather | solution.py:89
  7.3 189.2 %reduce-scatter.2.cloned.1.call-start = ((), (), s32[]{:S(2)}) async-start(), calls=%async_computation.1 | async-start | bytes 2752512 | tf_op jit(solution)/shard_map/reduce_scatter | solution.py:92
  8.2 30.1 %collective-permute-start = (bf16[2,256,128]{2,1,0:T(8,128)(2,1)S(1)}, bf16[2,256,128]{2,1,0:T(8,128)(2,1)S(1)}, u32[]{:S(2)}, u32[]{:S(2)}) collective-permute-start(bf16[2,256,128]{2,1,0:T(8,128)(2,1)S(1)} %pad_maximum_fusion), channel_id=1, source_target_pairs={{0,2},{2,4},{4,6},{6,8},{8,10},{10,12},{12,14},{14,16},{16,18},{18... | collective-permute-start | bytes 393224 | tf_op jit(solution)/shard_map/ppermute | solution.py:24
  13.8 51.1 %collective-permute-start.8 = (bf16[2,256,128]{2,1,0:T(8,128)(2,1)S(1)}, bf16[2,256,128]{2,1,0:T(8,128)(2,1)S(1)}, u32[]{:S(2)}, u32[]{:S(2)}) collective-permute-start(bf16[2,256,128]{2,1,0:T(8,128)(2,1)S(1)} %pad_maximum_fusion), channel_id=1, source_target_pairs={{0,256},{2,258},{4,260},{6,262},{8,264},{10,266},{12,268},{14,270}... | collective-permute-start | bytes 393224 | tf_op jit(solution)/shard_map/ppermute | solution.py:33
  24.4 40.4 %collective-permute-start.7 = (bf16[2,256,128]{2,1,0:T(8,128)(2,1)S(1)}, bf16[2,256,128]{2,1,0:T(8,128)(2,1)S(1)}, u32[]{:S(2)}, u32[]{:S(2)}) collective-permute-start(bf16[2,256,128]{2,1,0:T(8,128)(2,1)S(1)} %pad_maximum_fusion), channel_id=1, source_target_pairs={{0,128},{2,130},{4,132},{6,134},{8,136},{10,138},{12,140},{14,142}... | collective-permute-start | bytes 393224 | tf_op jit(solution)/shard_map/ppermute | solution.py:33
  28.5 36.4 %collective-permute-start.6 = (bf16[2,256,128]{2,1,0:T(8,128)(2,1)S(1)}, bf16[2,256,128]{2,1,0:T(8,128)(2,1)S(1)}, u32[]{:S(2)}, u32[]{:S(2)}) collective-permute-start(bf16[2,256,128]{2,1,0:T(8,128)(2,1)S(1)} %pad_maximum_fusion), channel_id=1, source_target_pairs={{0,64},{2,66},{4,68},{6,70},{8,72},{10,74},{12,76},{14,78},{16,80}... | collective-permute-start | bytes 393224 | tf_op jit(solution)/shard_map/ppermute | solution.py:33
  31.6 19.8 %collective-permute-start.2 = (bf16[2,256,128]{2,1,0:T(8,128)(2,1)S(1)}, bf16[2,256,128]{2,1,0:T(8,128)(2,1)S(1)}, u32[]{:S(2)}, u32[]{:S(2)}) collective-permute-start(bf16[2,256,128]{2,1,0:T(8,128)(2,1)S(1)} %pad_maximum_fusion), channel_id=1, source_target_pairs={{0,4},{2,6},{4,0},{6,2},{8,12},{10,14},{12,8},{14,10},{16,20},{18,... | collective-permute-start | bytes 393224 | tf_op jit(solution)/shard_map/ppermute | solution.py:33
  38.3 8.6 %collective-permute-start.1 = (bf16[2,256,128]{2,1,0:T(8,128)(2,1)S(1)}, bf16[2,256,128]{2,1,0:T(8,128)(2,1)S(1)}, u32[]{:S(2)}, u32[]{:S(2)}) collective-permute-start(bf16[2,256,128]{2,1,0:T(8,128)(2,1)S(1)} %pad_maximum_fusion), channel_id=1, source_target_pairs={{2,0},{4,2},{6,4},{8,6},{10,8},{12,10},{14,12},{16,14},{18,16},{20... | collective-permute-start | bytes 393224 | tf_op jit(solution)/shard_map/ppermute | solution.py:25
  47.0 10.7 %collective-permute-start.3 = (bf16[2,256,128]{2,1,0:T(8,128)(2,1)S(1)}, bf16[2,256,128]{2,1,0:T(8,128)(2,1)S(1)}, u32[]{:S(2)}, u32[]{:S(2)}) collective-permute-start(bf16[2,256,128]{2,1,0:T(8,128)(2,1)S(1)} %pad_maximum_fusion), channel_id=1, source_target_pairs={{0,8},{2,10},{4,12},{6,14},{8,0},{10,2},{12,4},{14,6},{16,24},{18,... | collective-permute-start | bytes 393224 | tf_op jit(solution)/shard_map/ppermute | solution.py:33
  51.4 10.9 %collective-permute-start.4 = (bf16[2,256,128]{2,1,0:T(8,128)(2,1)S(1)}, bf16[2,256,128]{2,1,0:T(8,128)(2,1)S(1)}, u32[]{:S(2)}, u32[]{:S(2)}) collective-permute-start(bf16[2,256,128]{2,1,0:T(8,128)(2,1)S(1)} %pad_maximum_fusion), channel_id=1, source_target_pairs={{0,16},{2,18},{4,20},{6,22},{8,24},{10,26},{12,28},{14,30},{16,0},... | collective-permute-start | bytes 393224 | tf_op jit(solution)/shard_map/ppermute | solution.py:33
  57.6 7.2 %collective-permute-start.5 = (bf16[2,256,128]{2,1,0:T(8,128)(2,1)S(1)}, bf16[2,256,128]{2,1,0:T(8,128)(2,1)S(1)}, u32[]{:S(2)}, u32[]{:S(2)}) collective-permute-start(bf16[2,256,128]{2,1,0:T(8,128)(2,1)S(1)} %pad_maximum_fusion), channel_id=1, source_target_pairs={{0,32},{2,34},{4,36},{6,38},{8,40},{10,42},{12,44},{14,46},{16,48}... | collective-permute-start | bytes 393224 | tf_op jit(solution)/shard_map/ppermute | solution.py:33
Sparse Core Ops, SparseCore 0:
  11.8 134.9 all-gather.2
  163.9 32.5 reduce-scatter.1
where the time goes:
time: 204 us; the launch traced here: 203 us
  waiting for transfers between devices  114 us (56%)
  starting transfers between devices  42.8 us (21%)
  matrix products  15.5 us (8%)
  between operations  13.7 us (7%)
  local copies, waits for them, and re-layouts  12.5 us (6%)
  other arithmetic  4.57 us (2%)
    all_gather x1, waiting for transfers between devices, local(): lax.all_gather(out_weight, 'seq', axis=1, tiled=True)  68.3 us
    ppermute x7, starting transfers between devices, partner_2(): return lax.ppermute(value, axis, pairs)  35.2 us
    reduce_scatter x1, waiting for transfers between devices, local(): lax.psum_scatter(column_terms.astype(jnp.bfloat16), 'head', scatter_dimen...  32.7 us
    unnamed x14, local copies, waits for them, and re-layouts  12.1 us
    ppermute x1, waiting for transfers between devices, padded_2(): after = lax.ppermute(first, axis, down)  6.62 us
    dot_general x1, matrix products, local(): jnp.dot(results, lax.all_gather(out_weight, 'seq', axis=1, tiled=True), p...  6.2 us
    ppermute x7, waiting for transfers between devices, partner_2(): return lax.ppermute(value, axis, pairs)  5.69 us
    ppermute x1, starting transfers between devices, padded_2(): before = lax.ppermute(last, axis, up)  5.6 us
  transfers between devices with their start and end apart: 11, of which 5 were waited for; matrix products, arithmetic and copies ran while one was open for 8% of the time, Pallas kernels for 0%

commit v1 on v0

v1 whole, which is shorter than its diff:
```python
import functools
import math

import jax
import jax.numpy as jnp
from jax import lax
from jax.experimental import pallas as pl
from jax.experimental.pallas import tpu as pltpu
from jax.sharding import PartitionSpec as P

QPK = 7
HD = 128
BLK = 256
MESH = pl.DeviceIdType.MESH
NZ, NX, NY, NC = 4, 8, 4, 2
SEQ = NZ * NX * NY * NC
BITS = 8
SLOTS = BITS + 2
SHARD = 14
PACK = SHARD * NY * NC
ROWS = QPK * HD
FAR = 3


def body(
    q_hbm, k_hbm, v_hbm, w_hbm, out_ref,
    q_ref, kbuf, vbuf, shards, wbuf, s_ref, att, acc,
    load_sem, kv_send, kv_recv, sh_send, sh_recv, x_send, x_recv, xm_send, xm_recv,
    z_send, z_recv, zm_send, zm_recv, f_send, f_recv, fm_send, fm_recv, a_send, a_recv,
):
    seq = lax.axis_index("seq")
    head = lax.axis_index("head")
    core = seq % NC
    yh = (seq // NC) % NY
    x = (seq // (NC * NY)) % NX
    z = seq // (NC * NY * NX)
    d = 1 - 2 * core
    keep = (z // 2 + head) % 2 == 0

    def at(zz, xx, yy, cc):
        return ((zz % NZ * NX + xx % NX) * NY + yy % NY) * NC + cc % NC

    def flip(j):
        return seq + 2**j * (1 - 2 * ((seq // 2**j) % 2))

    kv_to = [(seq + 1) % SEQ, seq, (seq + SEQ - 1) % SEQ] + [flip(j) for j in range(1, BITS)]
    mate = at(z, x, yh, core + 1)
    x_next, x_prev = at(z, x + d + NX, yh, core), at(z, x - d + NX, yh, core)
    z_next, z_prev = at(z + d + NZ, x, yh, core), at(z - d + NZ, x, yh, core)

    away = 1 - ((z // 2 + head + 1) % 2)
    z_to = (z + 2 * away) % NZ
    head_to = (head + away) % 2
    sh_to = [at(z_to, x, yh + i // 2, core + i) for i in range(NY * NC)]

    loads = [
        pltpu.make_async_copy(q_hbm, q_ref, load_sem.at[0]),
        pltpu.make_async_copy(k_hbm, kbuf.at[1], load_sem.at[1]),
        pltpu.make_async_copy(v_hbm, vbuf.at[1], load_sem.at[2]),
    ]
    for copy in loads:
        copy.start()

    barrier = pltpu.get_barrier_semaphore()

    def greet(s, h):
        pl.semaphore_signal(barrier, inc=1, device_id=(s, h), device_id_type=MESH)

    for i in range(SLOTS):
        if i != 1:
            greet(kv_to[i], head)
    for s in (x_next, x_prev, z_next, z_prev):
        greet(s, head)
    greet(seq, 1 - head)
    for i in range(1, NY * NC):
        greet(sh_to[i], head_to)

    @pl.when(jnp.logical_not(keep))
    def _():
        greet(sh_to[0], head_to)

    pl.semaphore_wait(barrier, SLOTS - 1 + 5 + NY * NC - 1 + away)

    sent = []

    def remote(src, dst, send, recv, s, h=head):
        return pltpu.make_async_remote_copy(
            src_ref=src, dst_ref=dst, send_sem=send, recv_sem=recv, device_id=(s, h), device_id_type=MESH
        )

    def send(*args):
        copy = remote(*args)
        copy.start()
        sent.append(copy)

    mine = yh * NC + core
    sh_self = remote(w_hbm, shards.at[mine], sh_send.at[0], sh_recv.at[mine], sh_to[0], head_to)
    for i in range(1, NY * NC):
        send(w_hbm, shards.at[mine], sh_send.at[i], sh_recv.at[mine], sh_to[i], head_to)

    @pl.when(keep)
    def _():
        pltpu.make_async_copy(w_hbm, shards.at[mine], sh_recv.at[mine]).start()

    @pl.when(jnp.logical_not(keep))
    def _():
        sh_self.start()

    order = [0, 2, 3, 4, 5, 6, 7, 8, 9]
    for i in order:
        send(k_hbm, kbuf.at[i], kv_send.at[i, 0], kv_recv.at[i, 0], kv_to[i])
        send(v_hbm, vbuf.at[i], kv_send.at[i, 1], kv_recv.at[i, 1], kv_to[i])

    def chunk(zz, xx):
        zz = zz % NZ
        return wbuf.at[((zz // 2 + head) % 2) * 2 + zz % 2, xx % NX]

    def rel(a, dd):
        return [0, -dd, dd, -2 * dd, 2 * dd, -3 * dd, 3 * dd, 4][a] + x + NX

    def send_x(t):
        c = chunk(z, x - d * t + NX)
        send(c, c, x_send.at[t], x_recv.at[t], x_next)

    def wait_x(t):
        c = chunk(z, x - d * (t + 1) + NX)
        remote(c, c, x_send.at[t], x_recv.at[t], x_next).wait_recv()
        return c

    def mate_x(t):
        c = chunk(z, x - d * (t + 1) + NX)
        send(c, c, xm_send.at[t], xm_recv.at[t], mate)

    def wait_xm(t):
        c = chunk(z, x + d * (t + 1) + NX)
        remote(c, c, xm_send.at[t], xm_recv.at[t], mate).wait_recv()

    def send_z(a):
        c = chunk(z, rel(a, d))
        send(c, c, z_send.at[a], z_recv.at[a], z_next)

    def far_chunk(f, cc, dd):
        return x + 4 * cc if f == 0 else x - f * dd + NX

    def step_z(a):
        c = chunk(z - d + NZ, rel(a, d))
        remote(c, c, z_send.at[a], z_recv.at[a], z_next).wait_recv()
        if a in (1, 3, 5):
            f = (a + 1) // 2
            send(c, c, f_send.at[f], f_recv.at[f], z_next)
        if a in (0, 7):
            @pl.when(core == a // 7)
            def _():
                remote(c, c, f_send.at[0], f_recv.at[0], z_next).start()
        send(c, c, zm_send.at[a], zm_recv.at[a], mate)

    def wait_zm(a):
        c = chunk(z + d + NZ, rel(a, -d))
        remote(c, c, zm_send.at[a], zm_recv.at[a], mate).wait_recv()

    def step_f(f):
        c = chunk(z + 2, far_chunk(f, core, d))
        remote(c, c, f_send.at[f], f_recv.at[f], z_next).wait_recv()
        send(c, c, fm_send.at[f], fm_recv.at[f], mate)

    def wait_fm(f):
        c = chunk(z + 2, far_chunk(f, 1 - core, -d))
        remote(c, c, fm_send.at[f], fm_recv.at[f], mate).wait_recv()

    rate = (1.0 / math.sqrt(HD)) * math.log2(math.e)
    low = jnp.where(seq > 0, 3e38, -1e30).astype(jnp.float32)
    high = jnp.where(seq < SEQ - 1, 3e38, -1e30).astype(jnp.float32)

    def attend(h):
        cols = pl.ds(h * HD, HD)
        query = q_ref[:, cols]
        best = None
        for i in range(SLOTS):
            s = lax.dot_general(
                query, kbuf[i], (((1,), (1,)), ((), ())), preferred_element_type=jnp.float32
            )
            if i == 0:
                s = jnp.minimum(s, low)
            if i == 2:
                s = jnp.minimum(s, high)
            s_ref[:, i * BLK : (i + 1) * BLK] = s
            top = jnp.maximum(s[:, :HD], s[:, HD:])
            best = top if best is None else jnp.maximum(best, top)
        peak = jnp.max(best, axis=1, keepdims=True)
        total = jnp.zeros((BLK, HD), jnp.float32)
        blended = jnp.zeros((BLK, HD), jnp.float32)
        for i in range(SLOTS):
            w = jnp.exp2((s_ref[:, i * BLK : (i + 1) * BLK] - peak) * rate)
            total = total + w[:, :HD] + w[:, HD:]
            blended = blended + jnp.dot(
                w.astype(jnp.bfloat16), vbuf[i], preferred_element_type=jnp.float32
            )
        weight_sum = jnp.sum(total, axis=1, keepdims=True)
        att[0, :, cols] = (blended / weight_sum).astype(jnp.bfloat16)
        send(
            att.at[0, :, cols], att.at[1, :, cols], a_send.at[h], a_recv.at[h], seq, 1 - head
        )

    def wait_att(h):
        cols = pl.ds(h * HD, HD)
        remote(
            att.at[0, :, cols], att.at[1, :, cols], a_send.at[h], a_recv.at[h], seq, 1 - head
        ).wait_recv()

    def project(zz, first):
        zz = zz % NZ
        side = (zz // 2 + head) % 2
        w = wbuf[side * 2 + zz % 2].reshape(NX * PACK, ROWS)
        part = lax.dot_general(
            att[side], w, (((1,), (1,)), ((), ())), preferred_element_type=jnp.float32
        )
        if first:
            acc[zz % 2] = part
        else:
            acc[zz % 2] = acc[zz % 2] + part

    for i in range(NY * NC):
        remote(w_hbm, shards.at[i], sh_send.at[0], sh_recv.at[i], sh_to[0], head_to).wait_recv()
    own = chunk(z, x)
    rows = [shards[i].astype(jnp.float32) for i in range(NY * NC)]
    own[...] = jnp.concatenate(rows, axis=0).astype(jnp.bfloat16)

    def wait_kv(i):
        remote(k_hbm, kbuf.at[i], kv_send.at[i, 0], kv_recv.at[i, 0], kv_to[i]).wait_recv()
        remote(v_hbm, vbuf.at[i], kv_send.at[i, 1], kv_recv.at[i, 1], kv_to[i]).wait_recv()

    send_x(0)
    send_z(0)

    def hop_x(t):
        wait_x(t)
        if t < FAR:
            send_x(t + 1)
            mate_x(t)
            send_z(2 * t + 1)
        else:
            send_z(7)

    def side_x(t):
        wait_xm(t)
        send_z(2 * t + 2)

    for copy in loads:
        copy.wait()
    hop_x(0)
    side_x(0)
    step_z(0)
    hop_x(1)
    side_x(1)
    for i in order:
        wait_kv(i)
    attend(0)
    step_z(1)
    hop_x(2)
    side_x(2)
    attend(1)
    step_z(2)
    hop_x(3)
    attend(2)
    step_z(3)
    step_z(4)
    attend(3)
    step_z(5)
    attend(4)
    step_z(6)
    step_z(7)
    attend(5)
    step_f(1)
    attend(6)
    for h in range(QPK):
        wait_att(h)
    project(z, True)
    step_f(2)
    for a in range(8):
        wait_zm(a)
    project(z - d + NZ, True)
    step_f(3)
    step_f(0)
    project(z + d + NZ, False)
    for f in range(4):
        wait_fm(f)
    project(z + 2, False)
    out_ref[:, : NX * PACK] = acc[0].astype(jnp.bfloat16)
    out_ref[:, NX * PACK :] = acc[1].astype(jnp.bfloat16)

    for copy in sent:
        copy.wait_send()
    c = chunk(z - d + NZ, x + 4 * core)
    remote(c, c, f_send.at[0], f_recv.at[0], z_next).wait_send()

    @pl.when(jnp.logical_not(keep))
    def _():
        sh_self.wait_send()


def local(queries, key_rows, value_rows, out_weight):
    dma = pltpu.SemaphoreType.DMA
    f32, bf16 = jnp.float32, jnp.bfloat16
    shard_count = NY * NC
    return pl.pallas_call(
        body,
        out_shape=jax.ShapeDtypeStruct((BLK, 2 * NX * PACK), bf16),
        in_specs=[pl.BlockSpec(memory_space=pl.ANY)] * 4,
        out_specs=pl.BlockSpec(memory_space=pltpu.VMEM),
        scratch_shapes=[
            pltpu.VMEM((BLK, ROWS), bf16),
            pltpu.VMEM((SLOTS, BLK, HD), bf16),
            pltpu.VMEM((SLOTS, BLK, HD), bf16),
            pltpu.VMEM((shard_count, SHARD, ROWS), bf16),
            pltpu.VMEM((NZ, NX, PACK, ROWS), bf16),
            pltpu.VMEM((BLK, SLOTS * BLK), f32),
            pltpu.VMEM((2, BLK, ROWS), bf16),
            pltpu.VMEM((2, BLK, NX * PACK), f32),
            dma((3,)),
            dma((SLOTS, 2)), dma((SLOTS, 2)),
            dma((shard_count,)), dma((shard_count,)),
            dma((4,)), dma((4,)), dma((3,)), dma((3,)),
            dma((8,)), dma((8,)), dma((8,)), dma((8,)),
            dma((4,)), dma((4,)), dma((4,)), dma((4,)),
            dma((QPK,)), dma((QPK,)),
        ],
        compiler_params=pltpu.CompilerParams(
            collective_id=0, has_side_effects=True, vmem_limit_bytes=48 * 2**20
        ),
    )(queries, key_rows, value_rows, out_weight.T)


def solution(mesh):
    in_specs = (P("seq", "head"), P("seq", "head"), P("seq", "head"), P("head", "seq"))
    out_specs = P("seq", "head")
    return jax.shard_map(local, mesh=mesh, in_specs=in_specs, out_specs=out_specs, check_vma=False)
```

time: 204 us -> 116 us (0.57)
  the two profiles are of different devices: /device:TPU:1 before, /device:TPU:71 now
where the time goes in v1:
time: 116 us
  Pallas kernels  112 us (97%)
  local copies, waits for them, and re-layouts  4.37 us (4%)
    pallas_call x1, Pallas kernels, local(): pl.pallas_call(body, out_shape=jax.ShapeDtypeStruct((BLK, 2 * NX * PACK),...  112 us
    unnamed x9, local copies, waits for them, and re-layouts  4.37 us

profile of v1, /device:TPU:71, one launch (start us, length us, event | category | flops | bytes accessed | tf_op | source)
XLA Modules:
  0.0 116.0 jit_solution(14870926844680089121)
XLA Ops:
  0.0 0.0 copy-start
  0.0 1.0 copy-done
  1.0 0.0 copy-start.1
  1.0 0.8 copy-done.1
  1.9 0.0 copy-start.2
  1.9 0.8 copy-done.2
  2.7 0.0 copy-start.3
  2.7 0.7 copy-done.3
  3.4 111.6 %shard_map.46 = bf16[256,1792]{1,0:T(8,128)(2,1)S(1)} custom-call(bf16[256,896]{1,0:T(8,128)(2,1)S(1)} %copy-done, bf16[256,128]{1,0:T(8,128)(2,1)S(1)} %copy-done.1, bf16[256,128]{1,0:T(8,128)(2,1)S(1)} %copy-done.2, bf16[14,896]{1,0:T(8,128)(2,1)S(1)} %bitcast.1), custom_call_target="tpu_custom_call" | custom-call | tf_op jit(solution)/shard_map/pallas_call | solution.py:305
  115.1 0.9 copy.6
Async XLA Ops:
  0.0 1.0 copy-start
  1.0 0.8 copy-start.1
  1.9 0.8 copy-start.2
  2.7 0.7 copy-start.3

commit v2 on v1

v2 whole, which is shorter than its diff:
```python
import functools
import math

import jax
import jax.numpy as jnp
from jax import lax
from jax.experimental import pallas as pl
from jax.experimental.pallas import tpu as pltpu
from jax.sharding import PartitionSpec as P

QPK = 7
HD = 128
BLK = 256
MESH = pl.DeviceIdType.MESH
NZ, NX, NY, NC = 8, 4, 4, 2
HALF = NZ // 2
SEQ = NZ * NX * NY * NC
BITS = 8
SLOTS = BITS + 2
SHARD = 14
PACK = SHARD * NY * NC
ROWS = QPK * HD
FAR = 3
CUT = 5 * HD


def body(
    q_hbm, k_hbm, v_hbm, w_hbm, out_ref,
    q_ref, kbuf, vbuf, shards, wbuf, s_ref, att, acc,
    load_sem, kv_send, kv_recv, sh_send, sh_recv, z_send, z_recv, zm_send, zm_recv,
    x_send, x_recv, xm_send, xm_recv, f_send, f_recv, fm_send, fm_recv,
    q_send, q_recv, qm_send, qm_recv, t_send, t_recv, tm_send, tm_recv, a_send, a_recv,
):
    seq = lax.axis_index("seq")
    head = lax.axis_index("head")
    core = seq % NC
    yh = (seq // NC) % NY
    x = (seq // (NC * NY)) % NX
    z = seq // (NC * NY * NX)
    d = 1 - 2 * core
    keep = (z // HALF + head) % 2 == 0

    def at(zz, xx, yy, cc):
        return ((zz % NZ * NX + xx % NX) * NY + yy % NY) * NC + cc % NC

    def flip(j):
        return seq + 2**j * (1 - 2 * ((seq // 2**j) % 2))

    kv_to = [(seq + 1) % SEQ, seq, (seq + SEQ - 1) % SEQ] + [flip(j) for j in range(1, BITS)]
    mate = at(z, x, yh, core + 1)
    x_next, x_prev = at(z, x + d + NX, yh, core), at(z, x - d + NX, yh, core)
    z_next, z_prev = at(z + d + NZ, x, yh, core), at(z - d + NZ, x, yh, core)
    z_next2, z_prev2 = at(z + 2 * d + NZ, x, yh, core), at(z - 2 * d + NZ, x, yh, core)
    x_far = at(z, x + 2, yh, core)

    away = (z // HALF + head) % 2
    z_to = z + away * (NZ - 1 - 2 * z)
    head_to = (head + away) % 2
    sh_to = [at(z_to, x, yh + i // 2, core + i) for i in range(NY * NC)]

    loads = [
        pltpu.make_async_copy(q_hbm, q_ref, load_sem.at[0]),
        pltpu.make_async_copy(k_hbm, kbuf.at[1], load_sem.at[1]),
        pltpu.make_async_copy(v_hbm, vbuf.at[1], load_sem.at[2]),
    ]
    for copy in loads:
        copy.start()

    barrier = pltpu.get_barrier_semaphore()

    def greet(s, h):
        pl.semaphore_signal(barrier, inc=1, device_id=(s, h), device_id_type=MESH)

    for i in range(SLOTS):
        if i != 1:
            greet(kv_to[i], head)
    for s in (x_next, x_prev, z_next, z_prev, z_next2, z_prev2):
        greet(s, head)
    greet(seq, 1 - head)
    for i in range(1, NY * NC):
        greet(sh_to[i], head_to)

    @pl.when(jnp.logical_not(keep))
    def _():
        greet(sh_to[0], head_to)

    pl.semaphore_wait(barrier, SLOTS - 1 + 7 + NY * NC - 1 + away)

    sent = []

    def remote(src, dst, send, recv, s, h=head):
        return pltpu.make_async_remote_copy(
            src_ref=src, dst_ref=dst, send_sem=send, recv_sem=recv, device_id=(s, h), device_id_type=MESH
        )

    def send(*args):
        copy = remote(*args)
        copy.start()
        sent.append(copy)

    mine = yh * NC + core
    sh_self = remote(w_hbm, shards.at[mine], sh_send.at[0], sh_recv.at[mine], sh_to[0], head_to)
    for i in range(1, NY * NC):
        send(w_hbm, shards.at[mine], sh_send.at[i], sh_recv.at[mine], sh_to[i], head_to)

    @pl.when(keep)
    def _():
        pltpu.make_async_copy(w_hbm, shards.at[mine], sh_recv.at[mine]).start()

    @pl.when(jnp.logical_not(keep))
    def _():
        sh_self.start()

    order = [0, 2, 3, 4, 5, 6, 7, 8, 9]
    for i in order:
        send(k_hbm, kbuf.at[i], kv_send.at[i, 0], kv_recv.at[i, 0], kv_to[i])
        send(v_hbm, vbuf.at[i], kv_send.at[i, 1], kv_recv.at[i, 1], kv_to[i])

    def place(zz):
        side = ((zz % NZ) // HALF + head) % 2
        quarter = zz % HALF
        return side, quarter + side * (HALF - 1 - 2 * quarter)

    def chunk(zz, xx):
        side, quarter = place(zz)
        return wbuf.at[xx % NX, side, quarter, :, pl.ds(0, CUT)]

    def whole(zz, xx):
        side, quarter = place(zz)
        return wbuf.at[xx % NX, side, quarter]

    def tail(zz, xx):
        side, quarter = place(zz)
        return wbuf.at[xx % NX, side, quarter, :, pl.ds(CUT, ROWS - CUT)]

    def half_tail(zz, xx, cc):
        side, quarter = place(zz)
        lanes = pl.ds(pl.multiple_of(CUT + HD * cc, HD), HD)
        return wbuf.at[xx % NX, side, quarter, :, lanes]

    def tail_row(zz):
        side, quarter = place(zz)
        return wbuf.at[:, side, quarter, :, pl.ds(CUT, ROWS - CUT)]

    def rel(a, dd):
        return [0, -dd, dd, -2 * dd, 2 * dd, -3 * dd, 3 * dd, 4][a] + z + NZ

    even = z % 2 == core

    def z_copy(t, c):
        to = (z_next, z_next2, z_next, z_next2)[t]
        return remote(c, c, z_send.at[t], z_recv.at[t], to)

    def send_z(t):
        copy = z_copy(t, chunk(z, x))
        copy.start()
        sent.append(copy)

    def z_mate(t):
        c = chunk(z - d * (t + 1) + NZ, x)
        return remote(c, c, zm_send.at[t], zm_recv.at[t], mate)

    def hop_z(t):
        c = chunk(z - d * (t + 1) + NZ, x)
        if t == FAR:
            @pl.when(even)
            def _():
                z_copy(t, c).wait_recv()
                z_mate(t).start()

            return
        z_copy(t, c).wait_recv()
        if t == 1:
            @pl.when(even)
            def _():
                z_copy(3, c).start()

            copy = z_copy(2, c)
            copy.start()
            sent.append(copy)
        copy = z_mate(t)
        copy.start()
        sent.append(copy)
        send_x(2 * t + 1)

    def side_z(t):
        c = chunk(z + d * (t + 1) + NZ, x)
        copy = remote(c, c, zm_send.at[t], zm_recv.at[t], mate)
        if t == FAR:
            @pl.when(jnp.logical_not(even))
            def _():
                copy.wait_recv()

            send_x(7)
        else:
            copy.wait_recv()
            send_x(2 * t + 2)

    def send_x(a):
        c = chunk(rel(a, d), x)
        send(c, c, x_send.at[a], x_recv.at[a], x_next)

    def far_chunk(f, cc, dd):
        return z + 4 * cc if f == 0 else z - f * dd + NZ

    def step_x(a):
        c = chunk(rel(a, d), x - d + NX)
        remote(c, c, x_send.at[a], x_recv.at[a], x_next).wait_recv()
        if a in (1, 3, 5):
            f = (a + 1) // 2
            send(c, c, f_send.at[f], f_recv.at[f], x_next)
        if a in (0, 7):
            @pl.when(core == a // 7)
            def _():
                remote(c, c, f_send.at[0], f_recv.at[0], x_next).start()
        send(c, c, xm_send.at[a], xm_recv.at[a], mate)

    def wait_xm(a):
        c = chunk(rel(a, -d), x + d + NX)
        remote(c, c, xm_send.at[a], xm_recv.at[a], mate).wait_recv()

    def step_f(f):
        c = chunk(far_chunk(f, core, d), x + 2)
        remote(c, c, f_send.at[f], f_recv.at[f], x_next).wait_recv()
        send(c, c, fm_send.at[f], fm_recv.at[f], mate)

    def wait_fm(f):
        c = chunk(far_chunk(f, 1 - core, -d), x + 2)
        remote(c, c, fm_send.at[f], fm_recv.at[f], mate).wait_recv()

    def tail_own():
        c = tail(z, x)
        send(c, c, q_send.at[0], q_recv.at[0], x_next)
        half = half_tail(z, x, core)
        send(half, half, q_send.at[1], q_recv.at[1], x_far)

    def tail_1():
        c = tail(z, x - d + NX)
        remote(c, c, q_send.at[0], q_recv.at[0], x_next).wait_recv()
        send(c, c, qm_send.at[0], qm_recv.at[0], mate)

    def tail_2():
        half = half_tail(z, x + 2, core)
        remote(half, half, q_send.at[1], q_recv.at[1], x_far).wait_recv()
        send(half, half, qm_send.at[1], qm_recv.at[1], mate)

    def t_copy(t, c):
        to = (z_next, z_next2, z_next, z_next2)[t]
        return remote(c, c, t_send.at[t], t_recv.at[t], to)

    def t_mate(t):
        c = tail_row(z - d * (t + 1) + NZ)
        return remote(c, c, tm_send.at[t], tm_recv.at[t], mate)

    def tail_3():
        c = tail(z, x + d + NX)
        remote(c, c, qm_send.at[0], qm_recv.at[0], mate).wait_recv()
        half = half_tail(z, x + 2, 1 - core)
        remote(half, half, qm_send.at[1], qm_recv.at[1], mate).wait_recv()
        for t in (1, 0):
            copy = t_copy(t, tail_row(z))
            copy.start()
            sent.append(copy)

    def step_tail(t):
        c = tail_row(z - d * (t + 1) + NZ)
        if t == FAR:
            @pl.when(even)
            def _():
                t_copy(t, c).wait_recv()
                t_mate(t).start()

            return
        t_copy(t, c).wait_recv()
        if t == 1:
            @pl.when(even)
            def _():
                t_copy(3, c).start()

            copy = t_copy(2, c)
            copy.start()
            sent.append(copy)
        copy = t_mate(t)
        copy.start()
        sent.append(copy)

    def wait_tm(t):
        c = tail_row(z + d * (t + 1) + NZ)
        copy = remote(c, c, tm_send.at[t], tm_recv.at[t], mate)
        if t == FAR:
            @pl.when(jnp.logical_not(even))
            def _():
                copy.wait_recv()
        else:
            copy.wait_recv()

    rate = (1.0 / math.sqrt(HD)) * math.log2(math.e)
    low = jnp.where(seq > 0, 3e38, -1e30).astype(jnp.float32)
    high = jnp.where(seq < SEQ - 1, 3e38, -1e30).astype(jnp.float32)

    def attend(h):
        cols = pl.ds(h * HD, HD)
        query = q_ref[:, cols]
        best = None
        for i in range(SLOTS):
            s = lax.dot_general(
                query, kbuf[i], (((1,), (1,)), ((), ())), preferred_element_type=jnp.float32
            )
            if i == 0:
                s = jnp.minimum(s, low)
            if i == 2:
                s = jnp.minimum(s, high)
            s_ref[:, i * BLK : (i + 1) * BLK] = s
            top = jnp.maximum(s[:, :HD], s[:, HD:])
            best = top if best is None else jnp.maximum(best, top)
        peak = jnp.max(best, axis=1, keepdims=True)
        total = jnp.zeros((BLK, HD), jnp.float32)
        blended = jnp.zeros((BLK, HD), jnp.float32)
        for i in range(SLOTS):
            w = jnp.exp2((s_ref[:, i * BLK : (i + 1) * BLK] - peak) * rate)
            total = total + w[:, :HD] + w[:, HD:]
            blended = blended + jnp.dot(
                w.astype(jnp.bfloat16), vbuf[i], preferred_element_type=jnp.float32
            )
        weight_sum = jnp.sum(total, axis=1, keepdims=True)
        att[0, :, cols] = (blended / weight_sum).astype(jnp.bfloat16)
        send(
            att.at[0, :, cols], att.at[1, :, cols], a_send.at[h], a_recv.at[h], seq, 1 - head
        )

    def wait_att(h):
        cols = pl.ds(h * HD, HD)
        remote(
            att.at[0, :, cols], att.at[1, :, cols], a_send.at[h], a_recv.at[h], seq, 1 - head
        ).wait_recv()

    def project(xx):
        xx = xx % NX
        part = None
        for side in range(2):
            w = wbuf[xx, side].reshape(HALF * PACK, ROWS)
            term = lax.dot_general(
                att[side], w, (((1,), (1,)), ((), ())), preferred_element_type=jnp.float32
            )
            part = term if part is None else part + term
        acc[xx] = part

    for i in range(NY * NC):
        remote(w_hbm, shards.at[i], sh_send.at[0], sh_recv.at[i], sh_to[0], head_to).wait_recv()
    own = whole(z, x)
    rows = [shards[i].astype(jnp.float32) for i in range(NY * NC)]
    own[...] = jnp.concatenate(rows, axis=0).astype(jnp.bfloat16)

    def wait_kv(i):
        remote(k_hbm, kbuf.at[i], kv_send.at[i, 0], kv_recv.at[i, 0], kv_to[i]).wait_recv()
        remote(v_hbm, vbuf.at[i], kv_send.at[i, 1], kv_recv.at[i, 1], kv_to[i]).wait_recv()

    tail_own()
    send_z(1)
    send_z(0)
    send_x(0)
    tail_1()
    tail_2()
    step_x(0)
    tail_3()
    hop_z(1)
    hop_z(0)
    side_z(1)
    side_z(0)
    for copy in loads:
        copy.wait()
    for i in order:
        wait_kv(i)
    attend(0)
    step_x(3)
    attend(1)
    step_x(1)
    attend(2)
    step_tail(1)
    step_x(4)
    attend(3)
    step_x(2)
    step_tail(0)
    attend(4)
    step_f(2)
    hop_z(3)
    attend(5)
    step_f(1)
    hop_z(2)
    side_z(3)
    attend(6)
    side_z(2)
    step_tail(3)
    step_tail(2)
    step_x(5)
    step_x(7)
    step_x(6)
    step_f(3)
    step_f(0)
    for t in range(FAR + 1):
        wait_tm(t)
    for h in range(QPK):
        wait_att(h)
    project(x)
    project(x - d + NX)
    for a in range(8):
        wait_xm(a)
    project(x + d + NX)
    for f in range(4):
        wait_fm(f)
    project(x + 2)
    for zz in range(HALF):
        for xx in range(NX):
            at_col = (zz * NX + xx) * PACK
            out_ref[:, at_col : at_col + PACK] = acc[
                xx, :, zz * PACK : (zz + 1) * PACK
            ].astype(jnp.bfloat16)

    for copy in sent:
        copy.wait_send()
    c = chunk(z + 4 * core, x - d + NX)
    remote(c, c, f_send.at[0], f_recv.at[0], x_next).wait_send()

    @pl.when(even)
    def _():
        far = chunk(z - 2 * d + NZ, x)
        z_copy(FAR, far).wait_send()
        z_mate(FAR).wait_send()
        t_copy(FAR, tail_row(z - 2 * d + NZ)).wait_send()
        t_mate(FAR).wait_send()

    @pl.when(jnp.logical_not(keep))
    def _():
        sh_self.wait_send()


def local(queries, key_rows, value_rows, out_weight):
    dma = pltpu.SemaphoreType.DMA
    f32, bf16 = jnp.float32, jnp.bfloat16
    shard_count = NY * NC
    return pl.pallas_call(
        body,
        out_shape=jax.ShapeDtypeStruct((BLK, HALF * NX * PACK), bf16),
        in_specs=[pl.BlockSpec(memory_space=pltpu.MemorySpace.HBM)] * 4,
        out_specs=pl.BlockSpec(memory_space=pltpu.VMEM),
        scratch_shapes=[
            pltpu.VMEM((BLK, ROWS), bf16),
            pltpu.VMEM((SLOTS, BLK, HD), bf16),
            pltpu.VMEM((SLOTS, BLK, HD), bf16),
            pltpu.VMEM((shard_count, SHARD, ROWS), bf16),
            pltpu.VMEM((NX, 2, HALF, PACK, ROWS), bf16),
            pltpu.VMEM((BLK, SLOTS * BLK), f32),
            pltpu.VMEM((2, BLK, ROWS), bf16),
            pltpu.VMEM((NX, BLK, HALF * PACK), f32),
            dma((3,)),
            dma((SLOTS, 2)), dma((SLOTS, 2)),
            dma((shard_count,)), dma((shard_count,)),
            dma((4,)), dma((4,)), dma((4,)), dma((4,)),
            dma((8,)), dma((8,)), dma((8,)), dma((8,)),
            dma((4,)), dma((4,)), dma((4,)), dma((4,)),
            dma((2,)), dma((2,)), dma((2,)), dma((2,)),
            dma((4,)), dma((4,)), dma((4,)), dma((4,)),
            dma((QPK,)), dma((QPK,)),
        ],
        compiler_params=pltpu.CompilerParams(
            collective_id=0, has_side_effects=True, vmem_limit_bytes=60 * 1024 * 1024
        ),
    )(queries, key_rows, value_rows, out_weight.T)


def solution(mesh):
    in_specs = (P("seq", "head"), P("seq", "head"), P("seq", "head"), P("head", "seq"))
    out_specs = P("seq", "head")
    return jax.shard_map(local, mesh=mesh, in_specs=in_specs, out_specs=out_specs, check_vma=False)
```

time: 116 us -> 75.1 us (0.65)
  the two profiles are of different devices: /device:TPU:71 before, /device:TPU:1 now
where the time goes in v2:
time: 75.1 us; the launch traced here: 74.8 us
  Pallas kernels  72.7 us (97%)
  local copies, waits for them, and re-layouts  2.16 us (3%)
    pallas_call x1, Pallas kernels, local(): pl.pallas_call(body, out_shape=jax.ShapeDtypeStruct((BLK, HALF * NX * PAC...  72.7 us
    unnamed x1, local copies, waits for them, and re-layouts  2.16 us

profile of v2, /device:TPU:1, one launch (start us, length us, event | category | flops | bytes accessed | tf_op | source)
XLA Modules:
  0.0 74.8 jit_solution(8645903849498051331)
XLA Ops:
  0.0 72.7 %shard_map.46 = bf16[256,1792]{1,0:T(8,128)(2,1)} custom-call(bf16[256,896]{1,0:T(8,128)(2,1)} %q_hbm.1, bf16[256,128]{1,0:T(8,128)(2,1)} %k_hbm.1, bf16[256,128]{1,0:T(8,128)(2,1)} %v_hbm.1, bf16[14,896]{1,0:T(8,128)(2,1)} %bitcast.1), custom_call_target="tpu_custom_call" | custom-call | tf_op jit(solution)/shard_map/pallas_call | solution.py:441
  72.7 2.2 %copy.6 = bf16[256,1792]{1,0:T(8,128)(2,1)} copy(bf16[256,1792]{1,0:T(8,128)(2,1)} %shard_map.46) | data formatting | bytes 1835008

commit v3 on v2

--- a/solution.py
+++ b/solution.py
@@ -21,13 +21,13 @@
 PACK = SHARD * NY * NC
 ROWS = QPK * HD
 FAR = 3
-CUT = 5 * HD
+CUT = 6 * HD
 
 
 def body(
     q_hbm, k_hbm, v_hbm, w_hbm, out_ref,
     q_ref, kbuf, vbuf, shards, wbuf, s_ref, att, acc,
-    load_sem, kv_send, kv_recv, sh_send, sh_recv, z_send, z_recv, zm_send, zm_recv,
+    load_sem, kv_send, kv_recv, sh_send, sh_recv, shm_send, shm_recv, z_send, z_recv, zm_send, zm_recv,
     x_send, x_recv, xm_send, xm_recv, f_send, f_recv, fm_send, fm_recv,
     q_send, q_recv, qm_send, qm_recv, t_send, t_recv, tm_send, tm_recv, a_send, a_recv,
 ):
@@ -56,7 +56,7 @@
     away = (z // HALF + head) % 2
     z_to = z + away * (NZ - 1 - 2 * z)
     head_to = (head + away) % 2
-    sh_to = [at(z_to, x, yh + i // 2, core + i) for i in range(NY * NC)]
+    sh_to = [at(z_to, x, yh + i, core) for i in range(NY)]
 
     loads = [
         pltpu.make_async_copy(q_hbm, q_ref, load_sem.at[0]),
@@ -77,14 +77,14 @@
     for s in (x_next, x_prev, z_next, z_prev, z_next2, z_prev2):
         greet(s, head)
     greet(seq, 1 - head)
-    for i in range(1, NY * NC):
+    for i in range(1, NY):
         greet(sh_to[i], head_to)
 
     @pl.when(jnp.logical_not(keep))
     def _():
         greet(sh_to[0], head_to)
 
-    pl.semaphore_wait(barrier, SLOTS - 1 + 7 + NY * NC - 1 + away)
+    pl.semaphore_wait(barrier, SLOTS - 1 + 7 + NY - 1 + away)
 
     sent = []
 
@@ -100,7 +100,7 @@
 
     mine = yh * NC + core
     sh_self = remote(w_hbm, shards.at[mine], sh_send.at[0], sh_recv.at[mine], sh_to[0], head_to)
-    for i in range(1, NY * NC):
+    for i in range(1, NY):
         send(w_hbm, shards.at[mine], sh_send.at[i], sh_recv.at[mine], sh_to[i], head_to)
 
     @pl.when(keep)
@@ -111,10 +111,14 @@
     def _():
         sh_self.start()
 
-    order = [0, 2, 3, 4, 5, 6, 7, 8, 9]
-    for i in order:
+    order = [5, 6, 0, 2, 3, 4, 7, 8, 9]
+
+    def send_kv(i):
         send(k_hbm, kbuf.at[i], kv_send.at[i, 0], kv_recv.at[i, 0], kv_to[i])
         send(v_hbm, vbuf.at[i], kv_send.at[i, 1], kv_recv.at[i, 1], kv_to[i])
+
+    for i in order:
+        send_kv(i)
 
     def place(zz):
         side = ((zz % NZ) // HALF + head) % 2
@@ -132,11 +136,6 @@
     def tail(zz, xx):
         side, quarter = place(zz)
         return wbuf.at[xx % NX, side, quarter, :, pl.ds(CUT, ROWS - CUT)]
-
-    def half_tail(zz, xx, cc):
-        side, quarter = place(zz)
-        lanes = pl.ds(pl.multiple_of(CUT + HD * cc, HD), HD)
-        return wbuf.at[xx % NX, side, quarter, :, lanes]
 
     def tail_row(zz):
         side, quarter = place(zz)
@@ -231,8 +230,7 @@
     def tail_own():
         c = tail(z, x)
         send(c, c, q_send.at[0], q_recv.at[0], x_next)
-        half = half_tail(z, x, core)
-        send(half, half, q_send.at[1], q_recv.at[1], x_far)
+        send(c, c, q_send.at[1], q_recv.at[1], x_far)
 
     def tail_1():
         c = tail(z, x - d + NX)
@@ -240,9 +238,8 @@
         send(c, c, qm_send.at[0], qm_recv.at[0], mate)
 
     def tail_2():
-        half = half_tail(z, x + 2, core)
-        remote(half, half, q_send.at[1], q_recv.at[1], x_far).wait_recv()
-        send(half, half, qm_send.at[1], qm_recv.at[1], mate)
+        c = tail(z, x + 2)
+        remote(c, c, q_send.at[1], q_recv.at[1], x_far).wait_recv()
 
     def t_copy(t, c):
         to = (z_next, z_next2, z_next, z_next2)[t]
@@ -255,8 +252,6 @@
     def tail_3():
         c = tail(z, x + d + NX)
         remote(c, c, qm_send.at[0], qm_recv.at[0], mate).wait_recv()
-        half = half_tail(z, x + 2, 1 - core)
-        remote(half, half, qm_send.at[1], qm_recv.at[1], mate).wait_recv()
         for t in (1, 0):
             copy = t_copy(t, tail_row(z))
             copy.start()
@@ -345,8 +340,13 @@
             part = term if part is None else part + term
         acc[xx] = part
 
-    for i in range(NY * NC):
-        remote(w_hbm, shards.at[i], sh_send.at[0], sh_recv.at[i], sh_to[0], head_to).wait_recv()
+    for i in range(NY):
+        c = shards.at[(yh + i) % NY * NC + core]
+        remote(w_hbm, c, sh_send.at[0], sh_recv.at[(yh + i) % NY * NC + core], sh_to[0], head_to).wait_recv()
+        send(c, c, shm_send.at[i], shm_recv.at[i], mate)
+    for i in range(NY):
+        c = shards.at[(yh + i) % NY * NC + 1 - core]
+        remote(c, c, shm_send.at[i], shm_recv.at[i], mate).wait_recv()
     own = whole(z, x)
     rows = [shards[i].astype(jnp.float32) for i in range(NY * NC)]
     own[...] = jnp.concatenate(rows, axis=0).astype(jnp.bfloat16)
@@ -361,37 +361,37 @@
     send_x(0)
     tail_1()
     tail_2()
+    tail_3()
     step_x(0)
-    tail_3()
-    hop_z(1)
-    hop_z(0)
-    side_z(1)
-    side_z(0)
     for copy in loads:
         copy.wait()
     for i in order:
         wait_kv(i)
     attend(0)
+    hop_z(1)
+    attend(1)
+    hop_z(0)
+    side_z(1)
+    attend(2)
+    side_z(0)
+    attend(3)
     step_x(3)
-    attend(1)
-    step_x(1)
-    attend(2)
     step_tail(1)
-    step_x(4)
-    attend(3)
-    step_x(2)
     step_tail(0)
     attend(4)
-    step_f(2)
+    step_x(1)
+    attend(5)
     hop_z(3)
-    attend(5)
-    step_f(1)
+    step_x(4)
+    attend(6)
     hop_z(2)
     side_z(3)
-    attend(6)
+    step_x(2)
+    step_tail(3)
     side_z(2)
-    step_tail(3)
     step_tail(2)
+    step_f(2)
+    step_f(1)
     step_x(5)
     step_x(7)
     step_x(6)
@@ -454,11 +454,11 @@
             pltpu.VMEM((NX, BLK, HALF * PACK), f32),
             dma((3,)),
             dma((SLOTS, 2)), dma((SLOTS, 2)),
-            dma((shard_count,)), dma((shard_count,)),
+            dma((NY,)), dma((shard_count,)), dma((NY,)), dma((NY,)),
             dma((4,)), dma((4,)), dma((4,)), dma((4,)),
             dma((8,)), dma((8,)), dma((8,)), dma((8,)),
             dma((4,)), dma((4,)), dma((4,)), dma((4,)),
-            dma((2,)), dma((2,)), dma((2,)), dma((2,)),
+            dma((2,)), dma((2,)), dma((1,)), dma((1,)),
             dma((4,)), dma((4,)), dma((4,)), dma((4,)),
             dma((QPK,)), dma((QPK,)),
         ],

time: 75.1 us -> 66.6 us (0.89)
  Pallas kernels: 72.7 us -> 64.1 us
    pallas_call x1, Pallas kernels: 72.7 us -> 64.1 us  [local(): pl.pallas_call(body, out_shape=jax.ShapeDtypeStruct((BLK, HALF * NX * PAC...]
where the time goes in v3:
time: 66.6 us; the launch traced here: 66.3 us
  Pallas kernels  64.1 us (96%)
  local copies, waits for them, and re-layouts  2.16 us (3%)
    pallas_call x1, Pallas kernels, local(): pl.pallas_call(body, out_shape=jax.ShapeDtypeStruct((BLK, HALF * NX * PAC...  64.1 us
    unnamed x1, local copies, waits for them, and re-layouts  2.16 us

profile of v3, /device:TPU:1, one launch (start us, length us, event | category | flops | bytes accessed | tf_op | source)
XLA Modules:
  0.0 66.3 jit_solution(8225123109274227564)
XLA Ops:
  0.0 64.1 %shard_map.46 = bf16[256,1792]{1,0:T(8,128)(2,1)} custom-call(bf16[256,896]{1,0:T(8,128)(2,1)} %q_hbm.1, bf16[256,128]{1,0:T(8,128)(2,1)} %k_hbm.1, bf16[256,128]{1,0:T(8,128)(2,1)} %v_hbm.1, bf16[14,896]{1,0:T(8,128)(2,1)} %bitcast.1), custom_call_target="tpu_custom_call" | custom-call | tf_op jit(solution)/shard_map/pallas_call | solution.py:441
  64.1 2.2 %copy.6 = bf16[256,1792]{1,0:T(8,128)(2,1)} copy(bf16[256,1792]{1,0:T(8,128)(2,1)} %shard_map.46) | data formatting | bytes 1835008

commit v4 on v3

--- a/solution.py
+++ b/solution.py
@@ -363,35 +363,35 @@
     tail_2()
     tail_3()
     step_x(0)
+    hop_z(1)
+    hop_z(0)
+    side_z(1)
+    side_z(0)
     for copy in loads:
         copy.wait()
     for i in order:
         wait_kv(i)
     attend(0)
-    hop_z(1)
-    attend(1)
-    hop_z(0)
-    side_z(1)
-    attend(2)
-    side_z(0)
-    attend(3)
     step_x(3)
     step_tail(1)
     step_tail(0)
-    attend(4)
+    attend(1)
     step_x(1)
-    attend(5)
+    attend(2)
     hop_z(3)
     step_x(4)
+    attend(3)
+    hop_z(2)
+    step_x(2)
+    side_z(3)
+    attend(4)
+    step_tail(3)
+    step_tail(2)
+    side_z(2)
+    step_f(2)
+    attend(5)
+    step_f(1)
     attend(6)
-    hop_z(2)
-    side_z(3)
-    step_x(2)
-    step_tail(3)
-    side_z(2)
-    step_tail(2)
-    step_f(2)
-    step_f(1)
     step_x(5)
     step_x(7)
     step_x(6)

time: 66.6 us -> 66.6 us (level)
  no operation moved by 1% of the time
where the time goes in v4:
time: 66.6 us; the launch traced here: 66.3 us
  Pallas kernels  64.1 us (96%)
  local copies, waits for them, and re-layouts  2.16 us (3%)
    pallas_call x1, Pallas kernels, local(): pl.pallas_call(body, out_shape=jax.ShapeDtypeStruct((BLK, HALF * NX * PAC...  64.1 us
    unnamed x1, local copies, waits for them, and re-layouts  2.16 us

profile of v4, /device:TPU:1, one launch (start us, length us, event | category | flops | bytes accessed | tf_op | source)
XLA Modules:
  0.0 66.3 jit_solution(4963395289485158028)
XLA Ops:
  0.0 64.1 %shard_map.46 = bf16[256,1792]{1,0:T(8,128)(2,1)} custom-call(bf16[256,896]{1,0:T(8,128)(2,1)} %q_hbm.1, bf16[256,128]{1,0:T(8,128)(2,1)} %k_hbm.1, bf16[256,128]{1,0:T(8,128)(2,1)} %v_hbm.1, bf16[14,896]{1,0:T(8,128)(2,1)} %bitcast.1), custom_call_target="tpu_custom_call" | custom-call | tf_op jit(solution)/shard_map/pallas_call | solution.py:441
  64.1 2.2 %copy.6 = bf16[256,1792]{1,0:T(8,128)(2,1)} copy(bf16[256,1792]{1,0:T(8,128)(2,1)} %shard_map.46) | data formatting | bytes 1835008
